TPU v7x, 32 devices: a whole 2x2x4 slice. The times are simulated.
32 devices in a mesh: chain: 4 (over x, core), col: 8 (over z, y).
Axes of the slice: x: 2, y: 2, z: 4, core: 2. Of those that a mesh axis runs over, the one named last changes fastest.
Arguments:
- rhs: float32 [4, 8, 64, 128], P('chain', 'col'), may hold values from -6 to 6
- inverse: float32 [4, 8, 128, 128], P('chain', 'col'), as said below
- factor: float32 [4, 8, 8, 128, 128], P('chain', 'col'), may hold values from -0.1875 to 0.1875
- pattern: int32 [4, 8, 8], P('chain', 'col'), may hold values from 0 to 7, as said below
Outputs:
- forward: float32 [4, 8, 64, 128], P('chain', 'col')
- solution: float32 [4, 8, 64, 128], P('chain', 'col')
Inputs may be any that keep to these rules, and one draw needn't show every extreme that they name: `pattern`: the 8 block rows of one supernode are distinct. `inverse`: each block is lower triangular, its diagonal between 0.5 and 1.5.
All inputs are finite; a program needn't handle non-finite values.
Results may differ from a plain program's by a relative error of at most 0.00012.
Values sent between devices are 32-bit elements; how exact they have to be, the bound alone decides.
A program may use at most 64 MiB of HBM per device.

v0:
```python
import functools

import jax
import jax.numpy as jnp
from jax import lax
from jax.experimental import pallas as pl
from jax.experimental.pallas import tpu as pltpu
from jax.sharding import PartitionSpec as P

PIECES = 4
MESH = pl.DeviceIdType.MESH


def halves(value):
    high = value.astype(jnp.bfloat16)
    low = (value - high.astype(jnp.float32)).astype(jnp.bfloat16)
    return high, low


def times_transposed(value, packed):
    rows = value.shape[0]
    high, low = halves(value)
    stacked = jnp.concatenate(
        [jnp.concatenate([high, low], axis=1), jnp.concatenate([low, high], axis=1)], axis=0
    )
    both = lax.dot_general(
        stacked, packed, (((1,), (1,)), ((), ())), preferred_element_type=jnp.float32
    )
    return both[:rows] + both[rows:]


def times_turned(value, turned):
    rows = value.shape[0]
    high, low = halves(value)
    stacked = jnp.concatenate(
        [jnp.concatenate([high, low], axis=1), jnp.concatenate([low, high], axis=1)], axis=0
    )
    both = jnp.dot(stacked, turned, preferred_element_type=jnp.float32)
    return both[:rows] + both[rows:]


def times(value, packed):
    rows = value.shape[0]
    width = packed.shape[1] // 2
    high, low = halves(value)
    both = jnp.dot(
        jnp.concatenate([high, low], axis=0), packed, preferred_element_type=jnp.float32
    )
    summed = both[:rows] + both[rows:]
    return summed[:, :width] + summed[:, width:]


def kernel(
    levels, supers, rhs_hbm, inverse_hbm, factor_hbm, pattern_hbm, both_ref,
    rhs, inverse, factor, pattern, inverse_packed, packed, turned, terms, outbox, inbox, solved,
    load_sem, outbox_sem, inbox_sem, solved_sem, arrived_sem, *arrived,
):
    forward_ref, answer_ref = both_ref.at[0], both_ref.at[1]
    place = lax.axis_index("chain")
    me = lax.axis_index("col")
    count, _, width = factor.shape
    loads = rhs.shape[0]
    rows = loads // PIECES
    loading = [
        pltpu.make_async_copy(source, target, load_sem.at[at])
        for at, (source, target) in enumerate(
            ((rhs_hbm, rhs), (inverse_hbm, inverse), (factor_hbm, factor), (pattern_hbm, pattern))
        )
    ]
    for copy in loading:
        copy.start()
    peers = [lax.rem(me + shift, supers) for shift in range(supers)]

    barrier = pltpu.get_barrier_semaphore()

    @pl.when(place > 0)
    def _():
        for peer in peers:
            pl.semaphore_signal(
                barrier, inc=1, device_id={"chain": place - 1, "col": peer}, device_id_type=MESH
            )

    @pl.when(place < levels - 1)
    def _():
        for peer in peers:
            pl.semaphore_signal(
                barrier, inc=1, device_id={"chain": place + 1, "col": peer}, device_id_type=MESH
            )

    loading[0].wait()
    loading[1].wait()
    high, low = halves(inverse[...])
    inverse_packed[:, :width] = high
    inverse_packed[:, width:] = low

    full = count == supers

    def pack(block, value):
        high, low = halves(value)
        packed[block * width:(block + 1) * width, :width] = high
        packed[block * width:(block + 1) * width, width:] = low

    def pack_turned(block, value):
        high, low = halves(value.T)
        turned[:width, block * width:(block + 1) * width] = high
        turned[width:, block * width:(block + 1) * width] = low

    def block_of(block):
        return factor[jnp.maximum(origin[block], 0)] if full else factor[block]

    loading[2].wait()
    loading[3].wait()
    targets = [pattern[0, 0, block] for block in range(count)]
    origin = []
    for peer in peers:
        at = jnp.int32(-1)
        for block in range(count):
            at = jnp.where(targets[block] == peer, jnp.int32(block), at)
        origin.append(at)
    slots = [lax.rem(me - target + supers, supers) for target in targets]

    @pl.when(place == 0)
    def _():
        for block in range(count):
            pack_turned(block, block_of(block))
        rhs[...] = times_transposed(rhs[...], inverse_packed[...])
        forward_ref[...] = rhs[...]

    @pl.when((place > 0) & (place < levels - 1))
    def _():
        for block in range(count):
            product = times(block_of(block), inverse_packed[...])
            pack(block, product)
            pack_turned(block, product)

    @pl.when(place == levels - 1)
    def _():
        pack(0, times(inverse[...].T, inverse_packed[...]))

    def term_copy(piece, shift):
        return pltpu.make_async_remote_copy(
            src_ref=outbox.at[piece, shift],
            dst_ref=inbox.at[piece, shift],
            send_sem=outbox_sem.at[piece, shift],
            recv_sem=inbox_sem.at[piece],
            device_id={"chain": place + 1, "col": peers[shift]},
            device_id_type=MESH,
        )

    def answer_copy(piece, shift):
        return pltpu.make_async_remote_copy(
            src_ref=solved.at[piece],
            dst_ref=arrived[piece].at[shift],
            send_sem=solved_sem.at[piece, shift],
            recv_sem=arrived_sem.at[piece],
            device_id={"chain": place - 1, "col": peers[shift]},
            device_id_type=MESH,
        )

    for piece in range(PIECES):
        part = pl.ds(piece * rows, rows)

        @pl.when(place > 0)
        def _():
            pltpu.make_async_copy(inbox.at[piece], inbox.at[piece], inbox_sem.at[piece]).wait()
            total = rhs[part, :] - jnp.sum(inbox[piece], axis=0)
            rhs[part, :] = total

        @pl.when(place < levels - 1)
        def _():
            wide = times_turned(rhs[part, :], turned[...])
            if full:
                for shift in range(supers):
                    outbox[piece, shift] = wide[:, shift * width:(shift + 1) * width]
            else:
                for block in range(count):
                    terms[block] = wide[:, block * width:(block + 1) * width]
                for shift in range(supers):
                    picked = terms[jnp.maximum(origin[shift], 0)]
                    outbox[piece, shift] = jnp.where(origin[shift] >= 0, picked, 0.0)

        @pl.when(place == levels - 1)
        def _():
            fresh = times(rhs[part, :], packed[:width, :])
            solved[piece] = fresh
            answer_ref[part, :] = fresh

        if piece == 0:
            pl.semaphore_wait(
                barrier, jnp.where(place > 0, supers, 0) + jnp.where(place < levels - 1, supers, 0)
            )

        @pl.when(place < levels - 1)
        def _():
            for shift in range(supers):
                term_copy(piece, shift).start()

        @pl.when(place == levels - 1)
        def _():
            for shift in range(supers):
                answer_copy(piece, shift).start()

    @pl.when(place > 0)
    def _():
        forward_ref[...] = times_transposed(rhs[...], inverse_packed[...])

    @pl.when(place == 0)
    def _():
        for block in range(count):
            pack(block, times(block_of(block), inverse_packed[...]))

    @pl.when(place < levels - 1)
    def _():
        rhs[...] = times(forward_ref[...], inverse_packed[...])
        for piece in range(PIECES):
            part = pl.ds(piece * rows, rows)
            pltpu.make_async_copy(arrived[piece], arrived[piece], arrived_sem.at[piece]).wait()
            if full:
                chosen = [arrived[piece][(supers - shift) % supers] for shift in range(supers)]
            else:
                chosen = [arrived[piece][slot] for slot in slots]
            picked = jnp.concatenate(chosen, axis=1)
            fresh = rhs[part, :] - times(picked, packed[...])
            solved[piece] = fresh
            answer_ref[part, :] = fresh

            @pl.when(place > 0)
            def _():
                for shift in range(supers):
                    answer_copy(piece, shift).start()

    @pl.when(place < levels - 1)
    def _():
        for piece in range(PIECES):
            for shift in range(supers):
                term_copy(piece, shift).wait_send()

    @pl.when(place > 0)
    def _():
        for piece in range(PIECES):
            for shift in range(supers):
                answer_copy(piece, shift).wait_send()


def body(rhs, inverse, factor, pattern):
    levels = lax.axis_size("chain")
    supers = lax.axis_size("col")
    loads, width = rhs.shape[2:]
    count = factor.shape[2]
    rows = loads // PIECES
    block = pltpu.VMEM((2, loads, width), jnp.float32)
    anywhere = pl.BlockSpec(memory_space=pl.ANY)
    both = pl.pallas_call(
        functools.partial(kernel, levels, supers),
        out_shape=block,
        in_specs=[anywhere] * 4,
        out_specs=pl.BlockSpec(memory_space=pltpu.VMEM),
        scratch_shapes=[
            pltpu.VMEM((loads, width), jnp.float32),
            pltpu.VMEM((width, width), jnp.float32),
            pltpu.VMEM((count, width, width), jnp.float32),
            pltpu.SMEM((1, 1, count), jnp.int32),
            pltpu.VMEM((width, 2 * width), jnp.bfloat16),
            pltpu.VMEM((count * width, 2 * width), jnp.bfloat16),
            pltpu.VMEM((2 * width, count * width), jnp.bfloat16),
            pltpu.VMEM((count, rows, width), jnp.float32),
            pltpu.VMEM((PIECES, supers, rows, width), jnp.float32),
            pltpu.VMEM((PIECES, supers, rows, width), jnp.float32),
            pltpu.VMEM((PIECES, rows, width), jnp.float32),
            pltpu.SemaphoreType.DMA((4,)),
            pltpu.SemaphoreType.DMA((PIECES, supers)),
            pltpu.SemaphoreType.DMA((PIECES,)),
            pltpu.SemaphoreType.DMA((PIECES, supers)),
            pltpu.SemaphoreType.DMA((PIECES,)),
            *[pltpu.VMEM((supers, rows, width), jnp.float32)] * PIECES,
        ],
        compiler_params=pltpu.CompilerParams(collective_id=0, has_side_effects=True),
    )(rhs[0, 0], inverse[0, 0], factor[0, 0], pattern)
    return (both[None, :1], both[None, 1:])


def solution(mesh):
    in_specs = (
        P("chain", "col", None, None),
        P("chain", "col", None, None),
        P("chain", "col", None, None, None),
        P("chain", "col", None),
    )
    out_specs = (P("chain", "col", None, None), P("chain", "col", None, None))
    return jax.shard_map(body, mesh=mesh, in_specs=in_specs, out_specs=out_specs, check_vma=False)
```

profile of v0, /device:TPU:0, one launch (start us, length us, event | category | flops | bytes accessed | tf_op | source)
XLA Modules:
  0.0 34.5 jit_solution(10891797575384116285)
XLA Ops:
  0.6 33.3 %shard_map.59 = f32[2,64,128]{2,1,0:T(8,128)S(1)} custom-call(f32[64,128]{1,0:T(8,128)} %bitcast.9, f32[128,128]{1,0:T(8,128)} %bitcast.8, f32[8,128,128]{2,1,0:T(8,128)} %bitcast.7, s32[1,1,8]{2,1,0:T(1,128)} %pattern_hbm.1), custom_call_target="tpu_custom_call" | custom-call | tf_op jit(solution)/shard_map/pallas_call | solution.py:253
  33.9 0.6 %slice_bitcast_fusion = (f32[1,1,64,128]{3,2,1,0:T(8,128)}, f32[1,1,64,128]{3,2,1,0:T(8,128)}) fusion(f32[2,64,128]{2,1,0:T(8,128)S(1)} %shard_map.59), kind=kLoop, calls=%fused_computation | loop fusion | bytes 131072 | tf_op jit(solution)/shard_map/broadcast_in_dim | solution.py:279
where the time goes:
time: 34.7 us; the launch traced here: 34.5 us
  Pallas kernels  33.3 us (96%)
  between operations  0.64 us (2%)
  local copies, waits for them, and re-layouts  0.63 us (2%)
    pallas_call x1, Pallas kernels, body(): pl.pallas_call(functools.partial(kernel, levels, supers), out_shape=block...  33.3 us

commit v1 on v0

--- a/solution.py
+++ b/solution.py
@@ -279,7 +279,470 @@
     return (both[None, :1], both[None, 1:])
 
 
+def spread_kernel(
+    supers, rhs_hbm, inverse_hbm, factor_hbm, pattern_hbm, both_ref,
+    rhs, inverse, factor, pattern, inverse_packed, packed, turned,
+    made, near1, near2, square1, square2, square3, side1, side2, side3,
+    turned1, packed1, turned2, packed2, mean1, mean2, mean3,
+    outbox, inbox1, inbox2, inbox3, inbox4, inbox5, held1, held2, held3, kept1, kept2, solved2, solved3,
+    back_u, back_x, back_pair,
+    load_sem, send_sem, near1_sem, near2_sem, square_sem, side_sem,
+    sem1, sem2, sem3, sem4, sem5, back_sem,
+):
+    forward_ref, answer_ref = both_ref.at[0], both_ref.at[1]
+    place = lax.axis_index("chain")
+    me = lax.axis_index("col")
+    depth = supers // 2
+    z, y = lax.div(me, 2), lax.rem(me, 2)
+    other = 1 - y
+    width = factor.shape[1]
+    rows = inbox1.shape[3]
+    half = 2 * rows
+    sends = []
+    count = send_sem.shape[0]
+    free = [None]
+    later = [None, None]
+
+    def at(chain, deep, side):
+        return {"chain": chain, "col": 2 * deep + side}
+
+    def remote(build, wanted=None):
+        index = next(free[0])
+
+        def make():
+            source, target, arrival, device = build()
+            return pltpu.make_async_remote_copy(
+                src_ref=source, dst_ref=target, send_sem=send_sem.at[index], recv_sem=arrival,
+                device_id=device, device_id_type=MESH,
+            )
+
+        if wanted is None:
+            make().start()
+        else:
+            pl.when(wanted())(lambda: make().start())
+        sends.append((make, wanted))
+
+    def take():
+        taken = list(sends)
+        sends.clear()
+        return taken
+
+    def finish(taken):
+        for make, wanted in taken:
+            if wanted is None:
+                make().wait_send()
+            else:
+                pl.when(wanted())(lambda make=make: make().wait_send())
+
+    def arrive(ref, sem):
+        pltpu.make_async_copy(ref, ref, sem).wait()
+
+    def rest(count):
+        step = 1 - 2 * lax.div(z, depth // 2)
+        return [lax.rem(z + step * k + count, count) for k in reversed(range(count))]
+
+    far = rest(depth)
+
+    def pack_into(ref, row, column, columns, value):
+        high, low = halves(value)
+        ref[row * width:(row + 1) * width, column * width:(column + 1) * width] = high
+        ref[row * width:(row + 1) * width, (columns + column) * width:(columns + column + 1) * width] = low
+
+    loading = [
+        pltpu.make_async_copy(source, target, load_sem.at[index])
+        for index, (source, target) in enumerate(
+            ((rhs_hbm, rhs), (inverse_hbm, inverse), (factor_hbm, factor), (pattern_hbm, pattern))
+        )
+    ]
+    for copy in loading:
+        copy.start()
+
+    barrier = pltpu.get_barrier_semaphore()
+
+    def greet(device, wanted=None):
+        def go():
+            pl.semaphore_signal(barrier, inc=1, device_id=device, device_id_type=MESH)
+
+        if wanted is None:
+            go()
+        else:
+            pl.when(wanted)(go)
+
+    @pl.when(place < 2)
+    def _():
+        for shift in range(supers):
+            peer = lax.rem(me + shift, supers)
+            greet({"chain": 0, "col": peer}, None if shift else place > 0)
+        greet(at(1, z, other))
+        greet(at(1, z, y), place == 0)
+        for deep in far:
+            greet(at(2, deep, y))
+        greet(at(3, z, y))
+        greet(at(3, z, other))
+
+    loading[1].wait()
+    high, low = halves(inverse[...])
+    inverse_packed[:, :width] = high
+    inverse_packed[:, width:] = low
+    loading[0].wait()
+    loading[2].wait()
+    loading[3].wait()
+    targets = [pattern[0, 0, block] for block in range(supers)]
+
+    def block_for(target):
+        found = jnp.int32(0)
+        for block in range(supers):
+            found = jnp.where(targets[block] == target, jnp.int32(block), found)
+        return factor[found]
+
+    def squared():
+        return times(inverse[...].T, inverse_packed[...])
+
+    @pl.when(place == 0)
+    def _():
+        free[0] = iter(range(count // 2))
+        for block in range(supers):
+            high, low = halves(block_for(block).T)
+            turned[:width, block * width:(block + 1) * width] = high
+            turned[width:, block * width:(block + 1) * width] = low
+        fresh = times_transposed(rhs[...], inverse_packed[...])
+        rhs[...] = fresh
+        forward_ref[...] = fresh
+        for piece in range(4):
+            q, c = piece // 2, piece % 2
+            part = slice(c * half + q * rows, c * half + (q + 1) * rows)
+            wide = times_turned(rhs[part, :], turned[...])
+            for deep in range(depth):
+                for side in range(2):
+                    block = 2 * deep + side
+                    outbox[piece, deep, side] = wide[:, block * width:(block + 1) * width]
+            if piece == 0:
+                pl.semaphore_wait(barrier, 2 * supers - 1)
+            if c == 0:
+                inbox1[q, me] = outbox[piece, z]
+            for deep in far:
+                for side in (other, y):
+                    remote(
+                        lambda piece=piece, q=q, c=c, deep=deep, side=side: (
+                            outbox.at[piece, deep], inbox1.at[q, me], sem1.at[q], at(c, deep, side)
+                        ),
+                        (lambda deep=deep: deep != z) if c == 0 and side is y else None,
+                    )
+        for block in range(supers):
+            product = times(block_for(block), inverse_packed[...])
+            high, low = halves(product)
+            packed[block * width:(block + 1) * width, :width] = high
+            packed[block * width:(block + 1) * width, width:] = low
+        for deep in range(depth):
+            arrive(near1.at[y, deep], near1_sem.at[y, deep])
+        later[0] = take()
+
+    @pl.when(place == 1)
+    def _():
+        free[0] = iter(range(count // 2))
+        pl.semaphore_wait(barrier, 3)
+        first, second = pl.ds(0, half), pl.ds(half, half)
+        remote(lambda: (rhs.at[first], side1.at[y], side_sem.at[0], at(0, z, y)))
+        remote(lambda: (rhs.at[first], side1.at[y], side_sem.at[0], at(0, z, other)))
+        remote(lambda: (rhs.at[second], side1.at[y], side_sem.at[0], at(1, z, other)))
+        side1[y] = rhs[second, :]
+        for deep in range(depth):
+            made[deep] = times(block_for(2 * deep + other), inverse_packed[...])
+            remote(lambda deep=deep: (made.at[deep], near1.at[y, deep], near1_sem.at[y, deep], at(1, z, other)))
+        for deep in range(depth):
+            near1[y, deep] = times(block_for(2 * deep + y), inverse_packed[...])
+            remote(lambda deep=deep: (near1.at[y, deep], near1.at[y, deep], near1_sem.at[y, deep], at(0, z, y)))
+        square1[...] = squared()
+        remote(lambda: (square1, square1, square_sem.at[0], at(0, z, y)))
+        for deep in range(depth):
+            arrive(near1.at[other, deep], near1_sem.at[other, deep])
+            remote(lambda deep=deep: (near1.at[other, deep], near1.at[other, deep], near1_sem.at[other, deep], at(0, z, y)))
+        later[1] = take()
+
+    @pl.when(place == 2)
+    def _():
+        free[0] = iter(range(count // 2))
+        for block in range(supers):
+            made[block] = times(block_for(block), inverse_packed[...])
+            if block == 0:
+                pl.semaphore_wait(barrier, supers)
+                for deep in far:
+                    for c in range(2):
+                        remote(lambda c=c, deep=deep: (rhs.at[pl.ds(c * half, half)], side2.at[z], side_sem.at[1], at(c, deep, y)))
+            deep, side = block // 2, block % 2
+            remote(lambda deep=deep, side=side, block=block: (made.at[block], near2.at[z, side], near2_sem.at[z, side], at(side, deep, y)))
+        square2[...] = squared()
+        for c in range(2):
+            remote(lambda c=c: (square2, square2, square_sem.at[1], at(c, z, y)))
+        finish(take())
+
+    @pl.when(place == 3)
+    def _():
+        free[0] = iter(range(count // 2))
+        square3[y] = squared()
+        pl.semaphore_wait(barrier, 4)
+        for c in range(2):
+            for side in (other, y):
+                remote(lambda c=c, side=side: (rhs.at[pl.ds(c * half, half)], side3.at[y], side_sem.at[2], at(c, z, side)))
+                remote(lambda c=c, side=side: (square3.at[y], square3.at[y], square_sem.at[2], at(c, z, side)))
+        finish(take())
+
+    @pl.when(place < 2)
+    def _():
+        free[0] = iter(range(count // 2, count))
+        @pl.when(place == 0)
+        def _():
+            for deep in range(depth):
+                arrive(near1.at[other, deep], near1_sem.at[other, deep])
+
+        for side in range(2):
+            for deep in range(depth):
+                value = near1[side, deep]
+                pack_into(turned1, side, deep, depth, value.T)
+                pack_into(packed1, deep, side, 2, value)
+
+        @pl.when(place == 0)
+        def _():
+            arrive(side1, side_sem.at[0])
+            arrive(square1, square_sem.at[0])
+
+        @pl.when(place == 1)
+        def _():
+            arrive(side1.at[0], side_sem.at[0])
+
+        pack_into(mean1, 0, 0, 1, square1[...])
+
+        for q in range(2):
+            part = slice(q * rows, (q + 1) * rows)
+
+            @pl.when(place == 0)
+            def _():
+                arrive(inbox1.at[q, pl.ds(0, supers - 1)], sem1.at[q])
+
+            @pl.when(place == 1)
+            def _():
+                arrive(inbox1.at[q], sem1.at[q])
+
+            for side in range(2):
+                held1[q, side] = side1[side, part, :] - jnp.sum(inbox1[q, :, side], axis=0)
+            wide = times(jnp.concatenate([held1[q, 0], held1[q, 1]], axis=1), turned1[...])
+            for deep in range(depth):
+                inbox2[q, z, deep] = wide[:, deep * width:(deep + 1) * width]
+            for deep in far[:-1]:
+                remote(lambda q=q, deep=deep: (inbox2.at[q, z], inbox2.at[q, z], sem2.at[q], at(place, deep, y)))
+            kept1[q] = times(held1[q, y], mean1[...])
+            remote(lambda q=q: (held1.at[q, y], back_u.at[2 * q], back_sem.at[0, q], at(1, z, y)), lambda: place == 0)
+
+            @pl.when(place == 1)
+            def _():
+                back_u[2 * q + 1] = held1[q, y]
+
+        for deep in range(depth):
+            arrive(near2.at[deep, place], near2_sem.at[deep, place])
+            remote(lambda deep=deep: (near2.at[deep, place], near2.at[deep, place], near2_sem.at[deep, place], at(1 - place, z, y)))
+        arrive(side2, side_sem.at[1])
+        arrive(square2, square_sem.at[1])
+        pack_into(mean2, 0, 0, 1, square2[...])
+        arrive(side3, side_sem.at[2])
+        arrive(square3, square_sem.at[2])
+        for side in range(2):
+            pack_into(mean3, side, 0, 1, square3[side])
+        for deep in range(depth):
+            arrive(near2.at[deep, 1 - place], near2_sem.at[deep, 1 - place])
+        for deep in range(depth):
+            for side in range(2):
+                value = near2[deep, side]
+                pack_into(turned2, deep, side, 2, value.T)
+                pack_into(packed2, side, deep, depth, value)
+
+        for q in range(2):
+            part = slice(q * rows, (q + 1) * rows)
+            arrive(inbox2.at[q, pl.ds(0, depth - 1)], sem2.at[q])
+            for deep in range(depth):
+                held2[q, deep] = side2[deep, part, :] - jnp.sum(inbox2[q, :, deep], axis=0)
+            wide = times(jnp.concatenate([held2[q, deep] for deep in range(depth)], axis=1), turned2[...])
+            for side in range(2):
+                inbox3[q, y, side] = wide[:, side * width:(side + 1) * width]
+            remote(lambda q=q: (inbox3.at[q, y], inbox3.at[q, y], sem3.at[q], at(place, z, other)))
+            kept2[q] = times(held2[q, z], mean2[...])
+            remote(lambda q=q: (held2.at[q, z], back_u.at[2 * q + place], back_sem.at[0, 2 * q + place], at(2, z, y)))
+
+        for q in range(2):
+            part = slice(q * rows, (q + 1) * rows)
+            arrive(inbox3.at[q, 0], sem3.at[q])
+            fresh = []
+            for side in range(2):
+                held3[q, side] = side3[side, part, :] - inbox3[q, 0, side] - inbox3[q, 1, side]
+                value = times(held3[q, side], mean3[side * width:(side + 1) * width, :])
+                solved3[q, side] = value
+                fresh.append(value)
+            wide = times(jnp.concatenate(fresh, axis=1), packed2[...])
+            for deep in range(depth):
+                inbox4[q, z, deep] = -wide[:, deep * width:(deep + 1) * width]
+            inbox4[q, z, z] = inbox4[q, z, z] + kept2[q]
+            for deep in far[:-1]:
+                remote(lambda q=q, deep=deep: (inbox4.at[q, z], inbox4.at[q, z], sem4.at[q], at(place, deep, y)))
+            remote(lambda q=q: (held3.at[q, y], back_u.at[2 * q + place], back_sem.at[0, 2 * q + place], at(3, z, y)))
+            remote(lambda q=q: (solved3.at[q, y], back_x.at[2 * q + place], back_sem.at[1, 2 * q + place], at(3, z, y)))
+
+        for q in range(2):
+            piece = 2 * q + place
+            arrive(inbox4.at[q, pl.ds(0, depth - 1)], sem4.at[q])
+            for deep in range(depth):
+                solved2[q, deep] = jnp.sum(inbox4[q, :, deep], axis=0)
+            wide = times(jnp.concatenate([solved2[q, deep] for deep in range(depth)], axis=1), packed1[...])
+            for side in range(2):
+                inbox5[piece, me, side] = -wide[:, side * width:(side + 1) * width]
+            inbox5[piece, me, y] = inbox5[piece, me, y] + kept1[q]
+            for deep in far:
+                for side in (other, y):
+                    remote(
+                        lambda q=q, deep=deep, side=side: (
+                            inbox5.at[2 * q + place, me], inbox5.at[2 * q + place, me],
+                            sem5.at[2 * q + place], at(0, deep, side)
+                        ),
+                        (lambda deep=deep: (deep != z) | (place != 0)) if side is y else None,
+                    )
+            remote(lambda q=q: (inbox5.at[2 * q + place, me, other], back_pair.at[2 * q + place, y], back_sem.at[1, 2 * q + place], at(1, z, other)))
+            remote(lambda q=q: (inbox5.at[2 * q + place, me, y], back_pair.at[2 * q + place, y], back_sem.at[1, 2 * q + place], at(1, z, y)), lambda: place == 0)
+
+            @pl.when(place == 1)
+            def _():
+                back_pair[piece, y] = inbox5[piece, me, y]
+
+            remote(lambda q=q: (solved2.at[q, z], back_x.at[2 * q + place], back_sem.at[1, 2 * q + place], at(2, z, y)))
+
+        @pl.when(place == 0)
+        def _():
+            rhs[...] = times(forward_ref[...], inverse_packed[...])
+            for piece in range(4):
+                q, c = piece // 2, piece % 2
+                part = slice(c * half + q * rows, c * half + (q + 1) * rows)
+                arrive(inbox5.at[piece, pl.ds(0, supers - 1 + c)], sem5.at[piece])
+                chosen = []
+                for deep in range(depth):
+                    for side in range(2):
+                        chosen.append(inbox5[piece, 2 * deep, side] + inbox5[piece, 2 * deep + 1, side])
+                answer_ref[part, :] = rhs[part, :] - times(jnp.concatenate(chosen, axis=1), packed[...])
+
+        finish(take())
+
+    for index in range(2):
+        @pl.when(place == index)
+        def _():
+            finish(later[index])
+
+    @pl.when(place > 0)
+    def _():
+        for piece in range(4):
+            q, c = piece // 2, piece % 2
+            part = slice(c * half + q * rows, c * half + (q + 1) * rows)
+            if c == 0:
+                @pl.when(place == 1)
+                def _():
+                    arrive(back_u.at[piece], back_sem.at[0, q])
+
+            @pl.when(place > 1)
+            def _():
+                arrive(back_u.at[piece], back_sem.at[0, piece])
+
+            rhs[part, :] = back_u[piece]
+        forward_ref[...] = times_transposed(rhs[...], inverse_packed[...])
+        for piece in range(4):
+            q, c = piece // 2, piece % 2
+            part = slice(c * half + q * rows, c * half + (q + 1) * rows)
+
+            @pl.when(place == 1)
+            def _():
+                arrive(back_pair.at[piece, pl.ds(0, 2 - c)], back_sem.at[1, piece])
+                answer_ref[part, :] = back_pair[piece, 0] + back_pair[piece, 1]
+
+            @pl.when(place > 1)
+            def _():
+                arrive(back_x.at[piece], back_sem.at[1, piece])
+                answer_ref[part, :] = back_x[piece]
+
+
+def spread_body(rhs, inverse, factor, pattern):
+    supers = lax.axis_size("col")
+    loads, width = rhs.shape[2:]
+    depth = supers // 2
+    rows, half = loads // 4, loads // 2
+    f32, bf16 = jnp.float32, jnp.bfloat16
+    square = (width, width)
+    piece = (rows, width)
+    anywhere = pl.BlockSpec(memory_space=pl.ANY)
+    dma = pltpu.SemaphoreType.DMA
+    both = pl.pallas_call(
+        functools.partial(spread_kernel, supers),
+        out_shape=pltpu.VMEM((2, loads, width), f32),
+        in_specs=[anywhere] * 4,
+        out_specs=pl.BlockSpec(memory_space=pltpu.VMEM),
+        scratch_shapes=[
+            pltpu.VMEM((loads, width), f32),
+            pltpu.VMEM(square, f32),
+            pltpu.VMEM((supers,) + square, f32),
+            pltpu.SMEM((1, 1, supers), jnp.int32),
+            pltpu.VMEM((width, 2 * width), bf16),
+            pltpu.VMEM((supers * width, 2 * width), bf16),
+            pltpu.VMEM((2 * width, supers * width), bf16),
+            pltpu.VMEM((supers,) + square, f32),
+            pltpu.VMEM((2, depth) + square, f32),
+            pltpu.VMEM((depth, 2) + square, f32),
+            pltpu.VMEM(square, f32),
+            pltpu.VMEM(square, f32),
+            pltpu.VMEM((2,) + square, f32),
+            pltpu.VMEM((2, half, width), f32),
+            pltpu.VMEM((depth, half, width), f32),
+            pltpu.VMEM((2, half, width), f32),
+            pltpu.VMEM((2 * width, 2 * depth * width), bf16),
+            pltpu.VMEM((depth * width, 4 * width), bf16),
+            pltpu.VMEM((depth * width, 4 * width), bf16),
+            pltpu.VMEM((2 * width, 2 * depth * width), bf16),
+            pltpu.VMEM((width, 2 * width), bf16),
+            pltpu.VMEM((width, 2 * width), bf16),
+            pltpu.VMEM((2 * width, 2 * width), bf16),
+            pltpu.VMEM((4, depth, 2) + piece, f32),
+            pltpu.VMEM((2, supers, 2) + piece, f32),
+            pltpu.VMEM((2, depth, depth) + piece, f32),
+            pltpu.VMEM((2, 2, 2) + piece, f32),
+            pltpu.VMEM((2, depth, depth) + piece, f32),
+            pltpu.VMEM((4, supers, 2) + piece, f32),
+            pltpu.VMEM((2, 2) + piece, f32),
+            pltpu.VMEM((2, depth) + piece, f32),
+            pltpu.VMEM((2, 2) + piece, f32),
+            pltpu.VMEM((2,) + piece, f32),
+            pltpu.VMEM((2,) + piece, f32),
+            pltpu.VMEM((2, depth) + piece, f32),
+            pltpu.VMEM((2, 2) + piece, f32),
+            pltpu.VMEM((4,) + piece, f32),
+            pltpu.VMEM((4,) + piece, f32),
+            pltpu.VMEM((4, 2) + piece, f32),
+            dma((4,)),
+            dma((160,)),
+            dma((2, depth)),
+            dma((depth, 2)),
+            dma((3,)),
+            dma((3,)),
+            dma((2,)),
+            dma((2,)),
+            dma((2,)),
+            dma((2,)),
+            dma((4,)),
+            dma((2, 4)),
+        ],
+        compiler_params=pltpu.CompilerParams(collective_id=0, has_side_effects=True),
+    )(rhs[0, 0], inverse[0, 0], factor[0, 0], pattern)
+    return (both[None, :1], both[None, 1:])
+
+
 def solution(mesh):
+    levels, supers = mesh.shape["chain"], mesh.shape["col"]
+
+    def chosen(rhs, inverse, factor, pattern):
+        dense = levels == 4 and factor.shape[2] == supers and supers % 4 == 0 and rhs.shape[2] % 32 == 0
+        return (spread_body if dense else body)(rhs, inverse, factor, pattern)
+
     in_specs = (
         P("chain", "col", None, None),
         P("chain", "col", None, None),
@@ -287,4 +750,4 @@
         P("chain", "col", None),
     )
     out_specs = (P("chain", "col", None, None), P("chain", "col", None, None))
-    return jax.shard_map(body, mesh=mesh, in_specs=in_specs, out_specs=out_specs, check_vma=False)
+    return jax.shard_map(chosen, mesh=mesh, in_specs=in_specs, out_specs=out_specs, check_vma=False)

time: 34.7 us -> 39.7 us (1.14)
  Pallas kernels: 33.3 us -> 38.3 us
    pallas_call x1, Pallas kernels: 33.3 us -> 38.3 us  [spread_body(): pl.pallas_call(functools.partial(spread_kernel, supers), out_shape=pltpu....]
where the time goes in v1:
time: 39.7 us; the launch traced here: 39.5 us
  Pallas kernels  38.3 us (96%)
  between operations  0.64 us (2%)
  local copies, waits for them, and re-layouts  0.63 us (2%)
    pallas_call x1, Pallas kernels, spread_body(): pl.pallas_call(functools.partial(spread_kernel, supers), out_shape=pltpu....  38.3 us

profile of v1, /device:TPU:0, one launch (start us, length us, event | category | flops | bytes accessed | tf_op | source)
XLA Modules:
  0.0 39.5 jit_solution(605617046773345744)
XLA Ops:
  0.6 38.3 %shard_map.59 = f32[2,64,128]{2,1,0:T(8,128)S(1)} custom-call(f32[64,128]{1,0:T(8,128)} %bitcast.9, f32[128,128]{1,0:T(8,128)} %bitcast.8, f32[8,128,128]{2,1,0:T(8,128)} %bitcast.7, s32[1,1,8]{2,1,0:T(1,128)} %pattern_hbm.1), custom_call_target="tpu_custom_call" | custom-call | tf_op jit(solution)/shard_map/pallas_call | solution.py:676
  38.9 0.6 %slice_bitcast_fusion = (f32[1,1,64,128]{3,2,1,0:T(8,128)}, f32[1,1,64,128]{3,2,1,0:T(8,128)}) fusion(f32[2,64,128]{2,1,0:T(8,128)S(1)} %shard_map.59), kind=kLoop, calls=%fused_computation | loop fusion | bytes 131072 | tf_op jit(solution)/shard_map/broadcast_in_dim | solution.py:736

commit v2 on v0

--- a/solution.py
+++ b/solution.py
@@ -70,6 +70,9 @@
     for copy in loading:
         copy.start()
     peers = [lax.rem(me + shift, supers) for shift in range(supers)]
+    upper = lax.div(2 * me, supers)
+    distant = [(1 - upper) * (supers - 1 - k) + upper * k for k in range(supers)]
+    distant = [(peer, lax.rem(peer - me + supers, supers)) for peer in distant]
 
     barrier = pltpu.get_barrier_semaphore()
 
@@ -137,23 +140,23 @@
     def _():
         pack(0, times(inverse[...].T, inverse_packed[...]))
 
-    def term_copy(piece, shift):
+    def term_copy(piece, peer, shift):
         return pltpu.make_async_remote_copy(
             src_ref=outbox.at[piece, shift],
             dst_ref=inbox.at[piece, shift],
             send_sem=outbox_sem.at[piece, shift],
             recv_sem=inbox_sem.at[piece],
-            device_id={"chain": place + 1, "col": peers[shift]},
+            device_id={"chain": place + 1, "col": peer},
             device_id_type=MESH,
         )
 
-    def answer_copy(piece, shift):
+    def answer_copy(piece, peer, shift):
         return pltpu.make_async_remote_copy(
             src_ref=solved.at[piece],
             dst_ref=arrived[piece].at[shift],
             send_sem=solved_sem.at[piece, shift],
             recv_sem=arrived_sem.at[piece],
-            device_id={"chain": place - 1, "col": peers[shift]},
+            device_id={"chain": place - 1, "col": peer},
             device_id_type=MESH,
         )
 
@@ -192,13 +195,13 @@
 
         @pl.when(place < levels - 1)
         def _():
-            for shift in range(supers):
-                term_copy(piece, shift).start()
+            for peer, shift in distant:
+                term_copy(piece, peer, shift).start()
 
         @pl.when(place == levels - 1)
         def _():
-            for shift in range(supers):
-                answer_copy(piece, shift).start()
+            for peer, shift in distant:
+                answer_copy(piece, peer, shift).start()
 
     @pl.when(place > 0)
     def _():
@@ -226,20 +229,20 @@
 
             @pl.when(place > 0)
             def _():
-                for shift in range(supers):
-                    answer_copy(piece, shift).start()
+                for peer, shift in distant:
+                    answer_copy(piece, peer, shift).start()
 
     @pl.when(place < levels - 1)
     def _():
         for piece in range(PIECES):
-            for shift in range(supers):
-                term_copy(piece, shift).wait_send()
+            for peer, shift in distant:
+                term_copy(piece, peer, shift).wait_send()
 
     @pl.when(place > 0)
     def _():
         for piece in range(PIECES):
-            for shift in range(supers):
-                answer_copy(piece, shift).wait_send()
+            for peer, shift in distant:
+                answer_copy(piece, peer, shift).wait_send()
 
 
 def body(rhs, inverse, factor, pattern):

time: 34.7 us -> 33.6 us (0.968)
  Pallas kernels: 33.3 us -> 32.2 us
    pallas_call x1, Pallas kernels: 33.3 us -> 32.2 us  [body(): pl.pallas_call(functools.partial(kernel, levels, supers), out_shape=block...]
where the time goes in v2:
time: 33.6 us; the launch traced here: 33.4 us
  Pallas kernels  32.2 us (96%)
  between operations  0.64 us (2%)
  local copies, waits for them, and re-layouts  0.63 us (2%)
    pallas_call x1, Pallas kernels, body(): pl.pallas_call(functools.partial(kernel, levels, supers), out_shape=block...  32.2 us

profile of v2, /device:TPU:0, one launch (start us, length us, event | category | flops | bytes accessed | tf_op | source)
XLA Modules:
  0.0 33.4 jit_solution(4953921699784752169)
XLA Ops:
  0.6 32.2 %shard_map.59 = f32[2,64,128]{2,1,0:T(8,128)S(1)} custom-call(f32[64,128]{1,0:T(8,128)} %bitcast.9, f32[128,128]{1,0:T(8,128)} %bitcast.8, f32[8,128,128]{2,1,0:T(8,128)} %bitcast.7, s32[1,1,8]{2,1,0:T(1,128)} %pattern_hbm.1), custom_call_target="tpu_custom_call" | custom-call | tf_op jit(solution)/shard_map/pallas_call | solution.py:256
  32.8 0.6 %slice_bitcast_fusion = (f32[1,1,64,128]{3,2,1,0:T(8,128)}, f32[1,1,64,128]{3,2,1,0:T(8,128)}) fusion(f32[2,64,128]{2,1,0:T(8,128)S(1)} %shard_map.59), kind=kLoop, calls=%fused_computation | loop fusion | bytes 131072 | tf_op jit(solution)/shard_map/broadcast_in_dim | solution.py:282

commit v3 on v2

--- a/solution.py
+++ b/solution.py
@@ -282,7 +282,387 @@
     return (both[None, :1], both[None, 1:])
 
 
+def folded_kernel(
+    levels, supers, rhs_hbm, inverse_hbm, factor_hbm, pattern_hbm, both_ref,
+    rhs, inverse, factor, pattern, inverse_packed, packed, turned, square, made,
+    outbox, inbox, inbox_top, arrived, arrived_top, solved, yout, back,
+    load_sem, send_sem, inbox_sem, top_sem, arrived_sem, back_top_sem, extra_sem, made_sem, back_sem,
+):
+    forward_ref, answer_ref = both_ref.at[0], both_ref.at[1]
+    place = lax.axis_index("chain")
+    me = lax.axis_index("col")
+    width = factor.shape[1]
+    rows = rhs.shape[1] // PIECES
+    below, top = levels - 2, levels - 1
+    depth = supers // 2
+    quarter = depth // 4
+    z, y = lax.div(me, 2), lax.rem(me, 2)
+    upper = lax.div(z, depth // 2)
+    middle = lax.rem(lax.div(lax.div(z, quarter) + 1, 2), 2)
+    mate = 2 * (z + (1 - 2 * middle) * quarter * (1 - 2 * upper)) + y
+    mate_chain = below + top - place
+    slot = lax.div(place, top)
+    first_id = me + (place - below) * (mate - me)
+    second_id = me + (top - place) * (mate - me)
+    works = (place >= below) & (middle == 1)
+    lends = (place >= below) & (middle == 0)
+    count = send_sem.shape[0]
+    sends = []
+    free = [None]
+    lent = []
+
+    def host(level, index):
+        deep, side = index // 2, index % 2
+        if level < below or quarter <= deep < 3 * quarter:
+            return level, index
+        deep += quarter if deep < quarter else -quarter
+        return below + top - level, 2 * deep + side
+
+    hosts = sorted({host(level, index) for level in (below, top) for index in range(supers)})
+
+    def away(device):
+        return (place != device[0]) | (me != device[1])
+
+    def copy_of(build, index):
+        source, target, arrival, device = build()
+        return pltpu.make_async_remote_copy(
+            src_ref=source, dst_ref=target, send_sem=send_sem.at[index], recv_sem=arrival,
+            device_id={"chain": device[0], "col": device[1]}, device_id_type=MESH,
+        )
+
+    def remote(build):
+        index = next(free[0])
+        copy_of(build, index).start()
+        sends.append((build, index, None))
+
+    def scatter(build, reached):
+        indices = [next(free[0]) for _ in range(supers)]
+
+        def start(item):
+            if reached(item) is None:
+                copy_of(lambda: build(item), indices[item]).start()
+            else:
+                pl.when(away(reached(item)))(lambda: copy_of(lambda: build(item), indices[item]).start())
+
+        for side in range(2):
+            @pl.when(upper == side)
+            def _():
+                for item in (range(supers) if side else reversed(range(supers))):
+                    start(item)
+
+        for item in range(supers):
+            sends.append((lambda item=item: build(item), indices[item], reached(item)))
+
+    def finish():
+        for build, index, device in sends:
+            if device is None:
+                copy_of(build, index).wait_send()
+            else:
+                pl.when(away(device))(lambda build=build, index=index: copy_of(build, index).wait_send())
+        sends.clear()
+
+    def arrive(ref, sem):
+        pltpu.make_async_copy(ref, ref, sem).wait()
+
+    def begin():
+        free[0] = iter(range(count))
+
+    def pack(block, value):
+        high, low = halves(value)
+        packed[block * width:(block + 1) * width, :width] = high
+        packed[block * width:(block + 1) * width, width:] = low
+
+    def pack_turned(block, value):
+        high, low = halves(value.T)
+        turned[:width, block * width:(block + 1) * width] = high
+        turned[width:, block * width:(block + 1) * width] = low
+
+    def pack_inverse(which):
+        high, low = halves(inverse[which])
+        inverse_packed[which, :, :width] = high
+        inverse_packed[which, :, width:] = low
+
+    loading = [
+        pltpu.make_async_copy(source, target, load_sem.at[at])
+        for at, (source, target) in enumerate(
+            (
+                (rhs_hbm, rhs.at[slot]), (inverse_hbm, inverse.at[slot]),
+                (factor_hbm, factor), (pattern_hbm, pattern),
+            )
+        )
+    ]
+    for copy in loading:
+        copy.start()
+
+    barrier = pltpu.get_barrier_semaphore()
+
+    def greet(chain, col):
+        pl.semaphore_signal(
+            barrier, inc=1, device_id={"chain": chain, "col": col}, device_id_type=MESH
+        )
+
+    peers = [lax.rem(me + shift, supers) for shift in range(supers)]
+
+    @pl.when((place > 0) & (place < below))
+    def _():
+        for peer in peers:
+            greet(place - 1, peer)
+
+    @pl.when(works)
+    def _():
+        greet(mate_chain, mate)
+        for peer in peers:
+            greet(below - 1, peer)
+        for chain, col in hosts:
+            pl.when(away((chain, col)))(lambda chain=chain, col=col: greet(chain, col))
+
+    @pl.when(lends)
+    def _():
+        begin()
+        pl.semaphore_wait(barrier, 1)
+        remote(lambda: (rhs_hbm, rhs.at[slot], extra_sem.at[0], (mate_chain, mate)))
+        remote(lambda: (inverse_hbm, inverse.at[slot], extra_sem.at[1], (mate_chain, mate)))
+        lent.extend(sends)
+        sends.clear()
+
+    loading[0].wait()
+    loading[1].wait()
+    pack_inverse(slot)
+    loading[2].wait()
+    loading[3].wait()
+    targets = [pattern[0, 0, block] for block in range(supers)]
+
+    def block_for(target):
+        found = jnp.int32(0)
+        for block in range(supers):
+            found = jnp.where(targets[block] == target, jnp.int32(block), found)
+        return factor[found]
+
+    def product(block):
+        return times(block_for(block), inverse_packed[0])
+
+    @pl.when(place == 0)
+    def _():
+        for block in range(supers):
+            pack_turned(block, block_for(block))
+        fresh = times_transposed(rhs[0], inverse_packed[0])
+        rhs[0] = fresh
+        forward_ref[...] = fresh
+
+    @pl.when(((place > 0) & (place < below)) | ((place == below) & works))
+    def _():
+        for block in range(supers):
+            value = product(block)
+            pack(block, value)
+            pack_turned(block, value)
+
+    @pl.when((place == below) & lends)
+    def _():
+        for block in range(supers):
+            made[block] = product(block)
+            remote(lambda block=block: (made.at[block], made.at[block], made_sem, (top, mate)))
+        finish()
+
+    @pl.when(lends)
+    def _():
+        sends.extend(lent)
+        finish()
+        arrive(back, back_sem.at[0])
+        forward_ref[...] = back[...]
+        arrive(solved.at[0], back_sem.at[1])
+        for piece in range(PIECES):
+            answer_ref[piece * rows:(piece + 1) * rows, :] = solved[0, piece]
+
+    def part_of(piece):
+        return slice(piece * rows, (piece + 1) * rows)
+
+    def spread(piece, value, level):
+        wide = times_turned(value, turned[...])
+        for block in range(supers):
+            outbox[piece, block] = wide[:, block * width:(block + 1) * width]
+        if level < below:
+            scatter(
+                lambda item, piece=piece: (
+                    outbox.at[piece, item], inbox.at[piece, me], inbox_sem.at[piece], host(level + 1, item)
+                ),
+                lambda item: None,
+            )
+        else:
+            @pl.when(works)
+            def _():
+                inbox_top[piece, first_id] = outbox[piece, second_id]
+
+            scatter(
+                lambda item, piece=piece: (
+                    outbox.at[piece, item], inbox_top.at[piece, first_id], top_sem.at[piece], host(top, item)
+                ),
+                lambda item: host(top, item),
+            )
+
+    def backward(piece, source, which):
+        picked = jnp.concatenate([source[block] for block in range(supers)], axis=1)
+        fresh = yout[which, part_of(piece), :] - times(picked, packed[...])
+        solved[which, piece] = fresh
+        return fresh
+
+    for level in range(below):
+        @pl.when(place == level)
+        def _():
+            begin()
+            for piece in range(PIECES):
+                if level > 0:
+                    arrive(inbox.at[piece], inbox_sem.at[piece])
+                    rhs[0, part_of(piece), :] = rhs[0, part_of(piece), :] - jnp.sum(inbox[piece], axis=0)
+                if piece == 0:
+                    pl.semaphore_wait(barrier, supers)
+                spread(piece, rhs[0, part_of(piece), :], level)
+            if level > 0:
+                forward_ref[...] = times_transposed(rhs[0], inverse_packed[0])
+            else:
+                for block in range(supers):
+                    pack(block, product(block))
+            yout[0] = times(forward_ref[...], inverse_packed[0])
+            for piece in range(PIECES):
+                arrive(arrived.at[piece], arrived_sem.at[piece])
+                answer_ref[part_of(piece), :] = backward(piece, arrived.at[piece], 0)
+                if level > 0:
+                    scatter(
+                        lambda item, piece=piece: (
+                            solved.at[0, piece], arrived.at[piece, me], arrived_sem.at[piece], (level - 1, item)
+                        ),
+                        lambda item: None,
+                    )
+            finish()
+
+    @pl.when(works)
+    def _():
+        begin()
+        which = 1 - slot
+        arrive(rhs.at[which], extra_sem.at[0])
+        arrive(inverse.at[which], extra_sem.at[1])
+        pack_inverse(which)
+        high, low = halves(times(inverse[1].T, inverse_packed[1]))
+        square[:, :width] = high
+        square[:, width:] = low
+
+        @pl.when(place == top)
+        def _():
+            arrive(made, made_sem)
+            for block in range(supers):
+                value = made[block]
+                pack(block, value)
+                pack_turned(block, value)
+
+        pl.semaphore_wait(barrier, supers - 1)
+        for piece in range(PIECES):
+            arrive(inbox.at[piece], inbox_sem.at[piece])
+            rhs[0, part_of(piece), :] = rhs[0, part_of(piece), :] - jnp.sum(inbox[piece], axis=0)
+            spread(piece, rhs[0, part_of(piece), :], below)
+        first = times_transposed(rhs[0], inverse_packed[0])
+        yout[0] = times(first, inverse_packed[0])
+
+        @pl.when(place == below)
+        def _():
+            forward_ref[...] = first
+
+        @pl.when(place == top)
+        def _():
+            back[...] = first
+
+        for piece in range(PIECES):
+            arrive(inbox_top.at[piece, pl.ds(0, supers - 1)], top_sem.at[piece])
+            total = rhs[1, part_of(piece), :] - jnp.sum(inbox_top[piece], axis=0)
+            rhs[1, part_of(piece), :] = total
+            fresh = times(total, square[...])
+            solved[1, piece] = fresh
+            arrived_top[piece, second_id] = fresh
+            scatter(
+                lambda item, piece=piece: (
+                    solved.at[1, piece], arrived_top.at[piece, second_id], back_top_sem.at[piece],
+                    host(below, item),
+                ),
+                lambda item: host(below, item),
+            )
+        second = times_transposed(rhs[1], inverse_packed[1])
+
+        @pl.when(place == below)
+        def _():
+            back[...] = second
+
+        @pl.when(place == top)
+        def _():
+            forward_ref[...] = second
+
+        remote(lambda: (back, back, back_sem.at[0], (mate_chain, mate)))
+        for piece in range(PIECES):
+            arrive(arrived_top.at[piece, pl.ds(0, supers - 1)], back_top_sem.at[piece])
+            backward(piece, arrived_top.at[piece], 0)
+            scatter(
+                lambda item, piece=piece: (
+                    solved.at[0, piece], arrived.at[piece, first_id], arrived_sem.at[piece], (below - 1, item)
+                ),
+                lambda item: None,
+            )
+        remote(lambda: (solved.at[which], solved.at[0], back_sem.at[1], (mate_chain, mate)))
+        for piece in range(PIECES):
+            answer_ref[part_of(piece), :] = solved[slot, piece]
+        finish()
+
+
+def folded_body(rhs, inverse, factor, pattern):
+    levels = lax.axis_size("chain")
+    supers = lax.axis_size("col")
+    loads, width = rhs.shape[2:]
+    rows = loads // PIECES
+    f32, bf16 = jnp.float32, jnp.bfloat16
+    piece = (rows, width)
+    dma = pltpu.SemaphoreType.DMA
+    anywhere = pl.BlockSpec(memory_space=pl.ANY)
+    both = pl.pallas_call(
+        functools.partial(folded_kernel, levels, supers),
+        out_shape=pltpu.VMEM((2, loads, width), f32),
+        in_specs=[anywhere] * 4,
+        out_specs=pl.BlockSpec(memory_space=pltpu.VMEM),
+        scratch_shapes=[
+            pltpu.VMEM((2, loads, width), f32),
+            pltpu.VMEM((2, width, width), f32),
+            pltpu.VMEM((supers, width, width), f32),
+            pltpu.SMEM((1, 1, supers), jnp.int32),
+            pltpu.VMEM((2, width, 2 * width), bf16),
+            pltpu.VMEM((supers * width, 2 * width), bf16),
+            pltpu.VMEM((2 * width, supers * width), bf16),
+            pltpu.VMEM((width, 2 * width), bf16),
+            pltpu.VMEM((supers, width, width), f32),
+            pltpu.VMEM((PIECES, supers) + piece, f32),
+            pltpu.VMEM((PIECES, supers) + piece, f32),
+            pltpu.VMEM((PIECES, supers) + piece, f32),
+            pltpu.VMEM((PIECES, supers) + piece, f32),
+            pltpu.VMEM((PIECES, supers) + piece, f32),
+            pltpu.VMEM((2, PIECES) + piece, f32),
+            pltpu.VMEM((2, loads, width), f32),
+            pltpu.VMEM((loads, width), f32),
+            dma((4,)),
+            dma((3 * PIECES * supers + 8,)),
+            dma((PIECES,)),
+            dma((PIECES,)),
+            dma((PIECES,)),
+            dma((PIECES,)),
+            dma((2,)),
+            dma(()),
+            dma((2,)),
+        ],
+        compiler_params=pltpu.CompilerParams(collective_id=0, has_side_effects=True),
+    )(rhs[0, 0], inverse[0, 0], factor[0, 0], pattern)
+    return (both[None, :1], both[None, 1:])
+
+
 def solution(mesh):
+    levels, supers = mesh.shape["chain"], mesh.shape["col"]
+
+    def chosen(rhs, inverse, factor, pattern):
+        dense = factor.shape[2] == supers and supers % 8 == 0 and levels > 2
+        return (folded_body if dense else body)(rhs, inverse, factor, pattern)
+
     in_specs = (
         P("chain", "col", None, None),
         P("chain", "col", None, None),
@@ -290,4 +670,4 @@
         P("chain", "col", None),
     )
     out_specs = (P("chain", "col", None, None), P("chain", "col", None, None))
-    return jax.shard_map(body, mesh=mesh, in_specs=in_specs, out_specs=out_specs, check_vma=False)
+    return jax.shard_map(chosen, mesh=mesh, in_specs=in_specs, out_specs=out_specs, check_vma=False)

time: 33.6 us -> 35.7 us (1.062)
  Pallas kernels: 32.2 us -> 34.3 us
    pallas_call x1, Pallas kernels: 32.2 us -> 34.3 us  [folded_body(): pl.pallas_call(functools.partial(folded_kernel, levels, supers), out_shap...]
where the time goes in v3:
time: 35.7 us; the launch traced here: 35.6 us
  Pallas kernels  34.3 us (96%)
  between operations  0.64 us (2%)
  local copies, waits for them, and re-layouts  0.63 us (2%)
    pallas_call x1, Pallas kernels, folded_body(): pl.pallas_call(functools.partial(folded_kernel, levels, supers), out_shap...  34.3 us

profile of v3, /device:TPU:0, one launch (start us, length us, event | category | flops | bytes accessed | tf_op | source)
XLA Modules:
  0.0 35.6 jit_solution(14961018862847142708)
XLA Ops:
  0.6 34.3 %shard_map.59 = f32[2,64,128]{2,1,0:T(8,128)S(1)} custom-call(f32[64,128]{1,0:T(8,128)} %bitcast.9, f32[128,128]{1,0:T(8,128)} %bitcast.8, f32[8,128,128]{2,1,0:T(8,128)} %bitcast.7, s32[1,1,8]{2,1,0:T(1,128)} %pattern_hbm.1), custom_call_target="tpu_custom_call" | custom-call | tf_op jit(solution)/shard_map/pallas_call | solution.py:621
  35.0 0.6 %slice_bitcast_fusion = (f32[1,1,64,128]{3,2,1,0:T(8,128)}, f32[1,1,64,128]{3,2,1,0:T(8,128)}) fusion(f32[2,64,128]{2,1,0:T(8,128)S(1)} %shard_map.59), kind=kLoop, calls=%fused_computation | loop fusion | bytes 131072 | tf_op jit(solution)/shard_map/broadcast_in_dim | solution.py:656

commit v4 on v2

--- a/solution.py
+++ b/solution.py
@@ -282,7 +282,335 @@
     return (both[None, :1], both[None, 1:])
 
 
+def inner_kernel(
+    levels, supers, rhs_hbm, inverse_hbm, factor_hbm, pattern_hbm, both_ref,
+    rhs, inverse, factor, pattern, inverse_packed, packed, turned, square,
+    outbox, inbox, inbox_top, arrived, solved, solved_top, back,
+    load_sem, outbox_sem, inbox_sem, solved_sem, arrived_sem, top_sem, lend_sem, extra_sem, back_sem,
+):
+    forward_ref, answer_ref = both_ref.at[0], both_ref.at[1]
+    place = lax.axis_index("chain")
+    me = lax.axis_index("col")
+    width = factor.shape[1]
+    rows = rhs.shape[1] // PIECES
+    below, top = levels - 2, levels - 1
+    depth = supers // 2
+    quarter = depth // 4
+    z, y = lax.div(me, 2), lax.rem(me, 2)
+    upper = lax.div(z, depth // 2)
+    middle = lax.rem(lax.div(lax.div(z, quarter) + 1, 2), 2)
+    mate = 2 * (z + (1 - 2 * middle) * quarter * (1 - 2 * upper)) + y
+    works = (place == top) & (middle == 1)
+    lends = (place == top) & (middle == 0)
+    order = []
+    for deep in range(quarter, 3 * quarter):
+        for side in range(2):
+            far = deep - quarter if deep < 2 * quarter else deep + quarter
+            order += [2 * deep + side, 2 * far + side]
+    is_below = lax.div(place, below) - lax.div(place, top)
+    mine = 2 * (me - 2 * quarter)
+
+    loading = [
+        pltpu.make_async_copy(source, target, load_sem.at[at])
+        for at, (source, target) in enumerate(
+            (
+                (rhs_hbm, rhs.at[0]), (inverse_hbm, inverse.at[0]),
+                (factor_hbm, factor), (pattern_hbm, pattern),
+            )
+        )
+    ]
+    for copy in loading:
+        copy.start()
+    peers = [lax.rem(me + shift, supers) for shift in range(supers)]
+    distant = [(1 - upper) * (supers - 1 - k) + upper * k for k in range(supers)]
+    near_top = []
+    for k in range(2 * quarter):
+        deep = (1 - upper) * (3 * quarter - 1 - k) + upper * (quarter + k)
+        for side in (1 - y, y):
+            near_top.append((2 * deep + side, 2 * (2 * (deep - quarter) + side)))
+
+    barrier = pltpu.get_barrier_semaphore()
+
+    def greet(chain, col):
+        pl.semaphore_signal(
+            barrier, inc=1, device_id={"chain": chain, "col": col}, device_id_type=MESH
+        )
+
+    @pl.when(((place > 0) & (place < top)) | works)
+    def _():
+        for peer in peers:
+            greet(place - 1, peer)
+
+    @pl.when(works)
+    def _():
+        greet(top, mate)
+
+    def lend(at):
+        return pltpu.make_async_remote_copy(
+            src_ref=(rhs_hbm, inverse_hbm)[at], dst_ref=(rhs, inverse)[at].at[1],
+            send_sem=lend_sem.at[at], recv_sem=extra_sem.at[at],
+            device_id={"chain": top, "col": mate}, device_id_type=MESH,
+        )
+
+    def give(at):
+        return pltpu.make_async_remote_copy(
+            src_ref=back.at[at], dst_ref=back.at[at],
+            send_sem=lend_sem.at[at], recv_sem=back_sem.at[at],
+            device_id={"chain": top, "col": mate}, device_id_type=MESH,
+        )
+
+    def arrive(ref, sem):
+        pltpu.make_async_copy(ref, ref, sem).wait()
+
+    @pl.when(lends)
+    def _():
+        pl.semaphore_wait(barrier, 1)
+        for at in range(2):
+            lend(at).start()
+
+    def pack_inverse(which):
+        high, low = halves(inverse[which])
+        inverse_packed[which, :, :width] = high
+        inverse_packed[which, :, width:] = low
+
+    loading[0].wait()
+    loading[1].wait()
+    pack_inverse(0)
+
+    def pack(block, value):
+        high, low = halves(value)
+        packed[block * width:(block + 1) * width, :width] = high
+        packed[block * width:(block + 1) * width, width:] = low
+
+    def pack_turned(block, value):
+        high, low = halves(value.T)
+        turned[:width, block * width:(block + 1) * width] = high
+        turned[width:, block * width:(block + 1) * width] = low
+
+    loading[2].wait()
+    loading[3].wait()
+    targets = [pattern[0, 0, block] for block in range(supers)]
+
+    def block_of(position):
+        wanted = position + (order[position] - position) * is_below
+        found = jnp.int32(0)
+        for block in range(supers):
+            found = jnp.where(targets[block] == wanted, jnp.int32(block), found)
+        return factor[found]
+
+    @pl.when(place == 0)
+    def _():
+        for block in range(supers):
+            pack_turned(block, block_of(block))
+        fresh = times_transposed(rhs[0], inverse_packed[0])
+        rhs[0] = fresh
+        forward_ref[...] = fresh
+
+    @pl.when((place > 0) & (place < top))
+    def _():
+        for block in range(supers):
+            product = times(block_of(block), inverse_packed[0])
+            pack(block, product)
+            pack_turned(block, product)
+
+    @pl.when(works)
+    def _():
+        for which in range(2):
+            if which:
+                arrive(rhs.at[1], extra_sem.at[0])
+                arrive(inverse.at[1], extra_sem.at[1])
+                pack_inverse(1)
+            high, low = halves(times(inverse[which].T, inverse_packed[which]))
+            square[which, :, :width] = high
+            square[which, :, width:] = low
+
+    def term_copy(piece, peer):
+        return pltpu.make_async_remote_copy(
+            src_ref=outbox.at[piece, peer], dst_ref=inbox.at[piece, me],
+            send_sem=outbox_sem.at[piece, peer], recv_sem=inbox_sem.at[piece],
+            device_id={"chain": place + 1, "col": peer}, device_id_type=MESH,
+        )
+
+    def top_copy(piece, col, start):
+        return pltpu.make_async_remote_copy(
+            src_ref=outbox.at[piece, pl.ds(start, 2)], dst_ref=inbox_top.at[piece, me],
+            send_sem=outbox_sem.at[piece, start], recv_sem=top_sem.at[piece],
+            device_id={"chain": top, "col": col}, device_id_type=MESH,
+        )
+
+    def answer_copy(piece, peer):
+        return pltpu.make_async_remote_copy(
+            src_ref=solved.at[piece], dst_ref=arrived.at[piece, me],
+            send_sem=solved_sem.at[piece, peer], recv_sem=arrived_sem.at[piece],
+            device_id={"chain": place - 1, "col": peer}, device_id_type=MESH,
+        )
+
+    def pair_copy(piece, peer):
+        return pltpu.make_async_remote_copy(
+            src_ref=solved_top.at[piece], dst_ref=arrived.at[piece, pl.ds(mine, 2)],
+            send_sem=solved_sem.at[piece, peer], recv_sem=arrived_sem.at[piece],
+            device_id={"chain": below, "col": peer}, device_id_type=MESH,
+        )
+
+    for piece in range(PIECES):
+        part = pl.ds(piece * rows, rows)
+
+        @pl.when((place > 0) & (place < top))
+        def _():
+            arrive(inbox.at[piece], inbox_sem.at[piece])
+            rhs[0, part, :] = rhs[0, part, :] - jnp.sum(inbox[piece], axis=0)
+
+        @pl.when(place < top)
+        def _():
+            wide = times_turned(rhs[0, part, :], turned[...])
+            for block in range(supers):
+                outbox[piece, block] = wide[:, block * width:(block + 1) * width]
+
+        if piece == 0:
+            @pl.when(place < top)
+            def _():
+                pl.semaphore_wait(barrier, supers - (supers // 2) * is_below)
+
+        @pl.when(place < below)
+        def _():
+            for peer in distant:
+                term_copy(piece, peer).start()
+
+        @pl.when(place == below)
+        def _():
+            for col, start in near_top:
+                top_copy(piece, col, start).start()
+
+        @pl.when(works)
+        def _():
+            arrive(inbox_top.at[piece], top_sem.at[piece])
+            for which in range(2):
+                total = rhs[which, part, :] - jnp.sum(inbox_top[piece, :, which], axis=0)
+                rhs[which, part, :] = total
+                solved_top[piece, which] = times(total, square[which])
+            for peer in distant:
+                pair_copy(piece, peer).start()
+
+    @pl.when((place > 0) & (place < top))
+    def _():
+        forward_ref[...] = times_transposed(rhs[0], inverse_packed[0])
+
+    @pl.when(place == 0)
+    def _():
+        for block in range(supers):
+            pack(block, times(block_of(block), inverse_packed[0]))
+
+    @pl.when(place < top)
+    def _():
+        rhs[0] = times(forward_ref[...], inverse_packed[0])
+        for piece in range(PIECES):
+            part = pl.ds(piece * rows, rows)
+            arrive(arrived.at[piece], arrived_sem.at[piece])
+            picked = jnp.concatenate([arrived[piece, block] for block in range(supers)], axis=1)
+            fresh = rhs[0, part, :] - times(picked, packed[...])
+            solved[piece] = fresh
+            answer_ref[part, :] = fresh
+
+            @pl.when(place > 0)
+            def _():
+                for peer in distant:
+                    answer_copy(piece, peer).start()
+
+    @pl.when(works)
+    def _():
+        back[0] = times_transposed(rhs[1], inverse_packed[1])
+        forward_ref[...] = times_transposed(rhs[0], inverse_packed[0])
+        for piece in range(PIECES):
+            part = pl.ds(piece * rows, rows)
+            answer_ref[part, :] = solved_top[piece, 0]
+            back[1, part, :] = solved_top[piece, 1]
+        for at in range(2):
+            give(at).start()
+        for piece in range(PIECES):
+            for peer in distant:
+                pair_copy(piece, peer).wait_send()
+        for at in range(2):
+            give(at).wait_send()
+
+    @pl.when(lends)
+    def _():
+        for at in range(2):
+            lend(at).wait_send()
+            arrive(back.at[at], back_sem.at[at])
+        forward_ref[...] = back[0]
+        answer_ref[...] = back[1]
+
+    @pl.when(place < below)
+    def _():
+        for piece in range(PIECES):
+            for peer in distant:
+                term_copy(piece, peer).wait_send()
+
+    @pl.when(place == below)
+    def _():
+        for piece in range(PIECES):
+            for col, start in near_top:
+                top_copy(piece, col, start).wait_send()
+
+    @pl.when((place > 0) & (place < top))
+    def _():
+        for piece in range(PIECES):
+            for peer in distant:
+                answer_copy(piece, peer).wait_send()
+
+
+def inner_body(rhs, inverse, factor, pattern):
+    levels = lax.axis_size("chain")
+    supers = lax.axis_size("col")
+    loads, width = rhs.shape[2:]
+    rows = loads // PIECES
+    f32, bf16 = jnp.float32, jnp.bfloat16
+    piece = (rows, width)
+    dma = pltpu.SemaphoreType.DMA
+    anywhere = pl.BlockSpec(memory_space=pl.ANY)
+    both = pl.pallas_call(
+        functools.partial(inner_kernel, levels, supers),
+        out_shape=pltpu.VMEM((2, loads, width), f32),
+        in_specs=[anywhere] * 4,
+        out_specs=pl.BlockSpec(memory_space=pltpu.VMEM),
+        scratch_shapes=[
+            pltpu.VMEM((2, loads, width), f32),
+            pltpu.VMEM((2, width, width), f32),
+            pltpu.VMEM((supers, width, width), f32),
+            pltpu.SMEM((1, 1, supers), jnp.int32),
+            pltpu.VMEM((2, width, 2 * width), bf16),
+            pltpu.VMEM((supers * width, 2 * width), bf16),
+            pltpu.VMEM((2 * width, supers * width), bf16),
+            pltpu.VMEM((2, width, 2 * width), bf16),
+            pltpu.VMEM((PIECES, supers) + piece, f32),
+            pltpu.VMEM((PIECES, supers) + piece, f32),
+            pltpu.VMEM((PIECES, supers, 2) + piece, f32),
+            pltpu.VMEM((PIECES, supers) + piece, f32),
+            pltpu.VMEM((PIECES,) + piece, f32),
+            pltpu.VMEM((PIECES, 2) + piece, f32),
+            pltpu.VMEM((2, loads, width), f32),
+            dma((4,)),
+            dma((PIECES, supers)),
+            dma((PIECES,)),
+            dma((PIECES, supers)),
+            dma((PIECES,)),
+            dma((PIECES,)),
+            dma((2,)),
+            dma((2,)),
+            dma((2,)),
+        ],
+        compiler_params=pltpu.CompilerParams(collective_id=0, has_side_effects=True),
+    )(rhs[0, 0], inverse[0, 0], factor[0, 0], pattern)
+    return (both[None, :1], both[None, 1:])
+
+
 def solution(mesh):
+    levels, supers = mesh.shape["chain"], mesh.shape["col"]
+
+    def chosen(rhs, inverse, factor, pattern):
+        dense = factor.shape[2] == supers and supers % 8 == 0 and levels > 3
+        return (inner_body if dense else body)(rhs, inverse, factor, pattern)
+
     in_specs = (
         P("chain", "col", None, None),
         P("chain", "col", None, None),
@@ -290,4 +618,4 @@
         P("chain", "col", None),
     )
     out_specs = (P("chain", "col", None, None), P("chain", "col", None, None))
-    return jax.shard_map(body, mesh=mesh, in_specs=in_specs, out_specs=out_specs, check_vma=False)
+    return jax.shard_map(chosen, mesh=mesh, in_specs=in_specs, out_specs=out_specs, check_vma=False)

time: 33.6 us -> 33.1 us (0.985)
  Pallas kernels: 32.2 us -> 31.7 us
    pallas_call x1, Pallas kernels: 32.2 us -> 31.7 us  [inner_body(): pl.pallas_call(functools.partial(inner_kernel, levels, supers), out_shape...]
where the time goes in v4:
time: 33.1 us; the launch traced here: 33 us
  Pallas kernels  31.7 us (96%)
  between operations  0.64 us (2%)
  local copies, waits for them, and re-layouts  0.63 us (2%)
    pallas_call x1, Pallas kernels, inner_body(): pl.pallas_call(functools.partial(inner_kernel, levels, supers), out_shape...  31.7 us

profile of v4, /device:TPU:0, one launch (start us, length us, event | category | flops | bytes accessed | tf_op | source)
XLA Modules:
  0.0 33.0 jit_solution(7684885863974806432)
XLA Ops:
  0.6 31.7 %shard_map.59 = f32[2,64,128]{2,1,0:T(8,128)S(1)} custom-call(f32[64,128]{1,0:T(8,128)} %bitcast.9, f32[128,128]{1,0:T(8,128)} %bitcast.8, f32[8,128,128]{2,1,0:T(8,128)} %bitcast.7, s32[1,1,8]{2,1,0:T(1,128)} %pattern_hbm.1), custom_call_target="tpu_custom_call" | custom-call | tf_op jit(solution)/shard_map/pallas_call | solution.py:571
  32.4 0.6 %slice_bitcast_fusion = (f32[1,1,64,128]{3,2,1,0:T(8,128)}, f32[1,1,64,128]{3,2,1,0:T(8,128)}) fusion(f32[2,64,128]{2,1,0:T(8,128)S(1)} %shard_map.59), kind=kLoop, calls=%fused_computation | loop fusion | bytes 131072 | tf_op jit(solution)/shard_map/broadcast_in_dim | solution.py:604

commit v5 on v4

--- a/solution.py
+++ b/solution.py
@@ -8,6 +8,7 @@
 from jax.sharding import PartitionSpec as P
 
 PIECES = 4
+EDGES = (0, 2, 5, 8)
 MESH = pl.DeviceIdType.MESH
 
 
@@ -292,7 +293,9 @@
     place = lax.axis_index("chain")
     me = lax.axis_index("col")
     width = factor.shape[1]
-    rows = rhs.shape[1] // PIECES
+    loads = rhs.shape[1]
+    edges = [loads * eighth // 8 for eighth in EDGES]
+    pieces = len(edges) - 1
     below, top = levels - 2, levels - 1
     depth = supers // 2
     quarter = depth // 4
@@ -322,7 +325,10 @@
     for copy in loading:
         copy.start()
     peers = [lax.rem(me + shift, supers) for shift in range(supers)]
-    distant = [(1 - upper) * (supers - 1 - k) + upper * k for k in range(supers)]
+    distant = []
+    for k in range(depth):
+        deep = (1 - upper) * (depth - 1 - k) + upper * k
+        distant += [2 * deep + 1 - y, 2 * deep + y]
     near_top = []
     for k in range(2 * quarter):
         deep = (1 - upper) * (3 * quarter - 1 - k) + upper * (quarter + k)
@@ -344,6 +350,9 @@
     @pl.when(works)
     def _():
         greet(top, mate)
+
+    def span(piece):
+        return pl.ds(edges[piece], edges[piece + 1] - edges[piece])
 
     def lend(at):
         return pltpu.make_async_remote_copy(
@@ -426,45 +435,45 @@
 
     def term_copy(piece, peer):
         return pltpu.make_async_remote_copy(
-            src_ref=outbox.at[piece, peer], dst_ref=inbox.at[piece, me],
+            src_ref=outbox.at[peer, span(piece)], dst_ref=inbox.at[me, span(piece)],
             send_sem=outbox_sem.at[piece, peer], recv_sem=inbox_sem.at[piece],
             device_id={"chain": place + 1, "col": peer}, device_id_type=MESH,
         )
 
     def top_copy(piece, col, start):
         return pltpu.make_async_remote_copy(
-            src_ref=outbox.at[piece, pl.ds(start, 2)], dst_ref=inbox_top.at[piece, me],
+            src_ref=outbox.at[pl.ds(start, 2), span(piece)], dst_ref=inbox_top.at[me, :, span(piece)],
             send_sem=outbox_sem.at[piece, start], recv_sem=top_sem.at[piece],
             device_id={"chain": top, "col": col}, device_id_type=MESH,
         )
 
     def answer_copy(piece, peer):
         return pltpu.make_async_remote_copy(
-            src_ref=solved.at[piece], dst_ref=arrived.at[piece, me],
+            src_ref=solved.at[span(piece)], dst_ref=arrived.at[me, span(piece)],
             send_sem=solved_sem.at[piece, peer], recv_sem=arrived_sem.at[piece],
             device_id={"chain": place - 1, "col": peer}, device_id_type=MESH,
         )
 
     def pair_copy(piece, peer):
         return pltpu.make_async_remote_copy(
-            src_ref=solved_top.at[piece], dst_ref=arrived.at[piece, pl.ds(mine, 2)],
+            src_ref=solved_top.at[:, span(piece)], dst_ref=arrived.at[pl.ds(mine, 2), span(piece)],
             send_sem=solved_sem.at[piece, peer], recv_sem=arrived_sem.at[piece],
             device_id={"chain": below, "col": peer}, device_id_type=MESH,
         )
 
-    for piece in range(PIECES):
-        part = pl.ds(piece * rows, rows)
+    for piece in range(pieces):
+        part = span(piece)
 
         @pl.when((place > 0) & (place < top))
         def _():
-            arrive(inbox.at[piece], inbox_sem.at[piece])
-            rhs[0, part, :] = rhs[0, part, :] - jnp.sum(inbox[piece], axis=0)
+            arrive(inbox.at[:, part], inbox_sem.at[piece])
+            rhs[0, part, :] = rhs[0, part, :] - jnp.sum(inbox[:, part, :], axis=0)
 
         @pl.when(place < top)
         def _():
             wide = times_turned(rhs[0, part, :], turned[...])
             for block in range(supers):
-                outbox[piece, block] = wide[:, block * width:(block + 1) * width]
+                outbox[block, part, :] = wide[:, block * width:(block + 1) * width]
 
         if piece == 0:
             @pl.when(place < top)
@@ -483,11 +492,11 @@
 
         @pl.when(works)
         def _():
-            arrive(inbox_top.at[piece], top_sem.at[piece])
+            arrive(inbox_top.at[:, :, part], top_sem.at[piece])
             for which in range(2):
-                total = rhs[which, part, :] - jnp.sum(inbox_top[piece, :, which], axis=0)
+                total = rhs[which, part, :] - jnp.sum(inbox_top[:, which, part, :], axis=0)
                 rhs[which, part, :] = total
-                solved_top[piece, which] = times(total, square[which])
+                solved_top[which, part, :] = times(total, square[which])
             for peer in distant:
                 pair_copy(piece, peer).start()
 
@@ -503,12 +512,12 @@
     @pl.when(place < top)
     def _():
         rhs[0] = times(forward_ref[...], inverse_packed[0])
-        for piece in range(PIECES):
-            part = pl.ds(piece * rows, rows)
-            arrive(arrived.at[piece], arrived_sem.at[piece])
-            picked = jnp.concatenate([arrived[piece, block] for block in range(supers)], axis=1)
+        for piece in range(pieces):
+            part = span(piece)
+            arrive(arrived.at[:, part], arrived_sem.at[piece])
+            picked = jnp.concatenate([arrived[block, part, :] for block in range(supers)], axis=1)
             fresh = rhs[0, part, :] - times(picked, packed[...])
-            solved[piece] = fresh
+            solved[part, :] = fresh
             answer_ref[part, :] = fresh
 
             @pl.when(place > 0)
@@ -520,13 +529,13 @@
     def _():
         back[0] = times_transposed(rhs[1], inverse_packed[1])
         forward_ref[...] = times_transposed(rhs[0], inverse_packed[0])
-        for piece in range(PIECES):
-            part = pl.ds(piece * rows, rows)
-            answer_ref[part, :] = solved_top[piece, 0]
-            back[1, part, :] = solved_top[piece, 1]
+        for piece in range(pieces):
+            part = span(piece)
+            answer_ref[part, :] = solved_top[0, part, :]
+            back[1, part, :] = solved_top[1, part, :]
         for at in range(2):
             give(at).start()
-        for piece in range(PIECES):
+        for piece in range(pieces):
             for peer in distant:
                 pair_copy(piece, peer).wait_send()
         for at in range(2):
@@ -542,19 +551,19 @@
 
     @pl.when(place < below)
     def _():
-        for piece in range(PIECES):
+        for piece in range(pieces):
             for peer in distant:
                 term_copy(piece, peer).wait_send()
 
     @pl.when(place == below)
     def _():
-        for piece in range(PIECES):
+        for piece in range(pieces):
             for col, start in near_top:
                 top_copy(piece, col, start).wait_send()
 
     @pl.when((place > 0) & (place < top))
     def _():
-        for piece in range(PIECES):
+        for piece in range(pieces):
             for peer in distant:
                 answer_copy(piece, peer).wait_send()
 
@@ -563,9 +572,9 @@
     levels = lax.axis_size("chain")
     supers = lax.axis_size("col")
     loads, width = rhs.shape[2:]
-    rows = loads // PIECES
+    pieces = len(EDGES) - 1
     f32, bf16 = jnp.float32, jnp.bfloat16
-    piece = (rows, width)
+    piece = (loads, width)
     dma = pltpu.SemaphoreType.DMA
     anywhere = pl.BlockSpec(memory_space=pl.ANY)
     both = pl.pallas_call(
@@ -582,19 +591,19 @@
             pltpu.VMEM((supers * width, 2 * width), bf16),
             pltpu.VMEM((2 * width, supers * width), bf16),
             pltpu.VMEM((2, width, 2 * width), bf16),
-            pltpu.VMEM((PIECES, supers) + piece, f32),
-            pltpu.VMEM((PIECES, supers) + piece, f32),
-            pltpu.VMEM((PIECES, supers, 2) + piece, f32),
-            pltpu.VMEM((PIECES, supers) + piece, f32),
-            pltpu.VMEM((PIECES,) + piece, f32),
-            pltpu.VMEM((PIECES, 2) + piece, f32),
+            pltpu.VMEM((supers,) + piece, f32),
+            pltpu.VMEM((supers,) + piece, f32),
+            pltpu.VMEM((supers, 2) + piece, f32),
+            pltpu.VMEM((supers,) + piece, f32),
+            pltpu.VMEM(piece, f32),
+            pltpu.VMEM((2,) + piece, f32),
             pltpu.VMEM((2, loads, width), f32),
             dma((4,)),
-            dma((PIECES, supers)),
-            dma((PIECES,)),
-            dma((PIECES, supers)),
-            dma((PIECES,)),
-            dma((PIECES,)),
+            dma((pieces, supers)),
+            dma((pieces,)),
+            dma((pieces, supers)),
+            dma((pieces,)),
+            dma((pieces,)),
             dma((2,)),
             dma((2,)),
             dma((2,)),
@@ -608,7 +617,7 @@
     levels, supers = mesh.shape["chain"], mesh.shape["col"]
 
     def chosen(rhs, inverse, factor, pattern):
-        dense = factor.shape[2] == supers and supers % 8 == 0 and levels > 3
+        dense = factor.shape[2] == supers and supers % 8 == 0 and rhs.shape[2] % 64 == 0 and levels > 3
         return (inner_body if dense else body)(rhs, inverse, factor, pattern)
 
     in_specs = (

time: 33.1 us -> 33 us (level)
  no operation moved by 1% of the time
where the time goes in v5:
time: 33 us; the launch traced here: 32.8 us
  Pallas kernels  31.6 us (96%)
  between operations  0.64 us (2%)
  local copies, waits for them, and re-layouts  0.63 us (2%)
    pallas_call x1, Pallas kernels, inner_body(): pl.pallas_call(functools.partial(inner_kernel, levels, supers), out_shape...  31.6 us

profile of v5, /device:TPU:0, one launch (start us, length us, event | category | flops | bytes accessed | tf_op | source)
XLA Modules:
  0.0 32.8 jit_solution(16145900282975920329)
XLA Ops:
  0.6 31.6 %shard_map.59 = f32[2,64,128]{2,1,0:T(8,128)S(1)} custom-call(f32[64,128]{1,0:T(8,128)} %bitcast.9, f32[128,128]{1,0:T(8,128)} %bitcast.8, f32[8,128,128]{2,1,0:T(8,128)} %bitcast.7, s32[1,1,8]{2,1,0:T(1,128)} %pattern_hbm.1), custom_call_target="tpu_custom_call" | custom-call | tf_op jit(solution)/shard_map/pallas_call | solution.py:580
  32.2 0.6 %slice_bitcast_fusion = (f32[1,1,64,128]{3,2,1,0:T(8,128)}, f32[1,1,64,128]{3,2,1,0:T(8,128)}) fusion(f32[2,64,128]{2,1,0:T(8,128)S(1)} %shard_map.59), kind=kLoop, calls=%fused_computation | loop fusion | bytes 131072 | tf_op jit(solution)/shard_map/broadcast_in_dim | solution.py:613
